TPU v7x, 128 devices: a whole 4x4x4 slice. The times are simulated.
128 devices in a mesh: gx: 16 (over x_lo, z, core), gy: 8 (over y, x_hi).
Axes of the slice: x: 4 (x_hi: 2, x_lo: 2; x = x_hi * 2 + x_lo), y: 4, z: 4, core: 2. Of those that a mesh axis runs over, the one named last changes fastest.
Arguments:
- features: bfloat16 [16, 8, 2048, 128], P('gx', 'gy'), may hold values from -96 to 96
- positions: float32 [16, 8, 3, 2048], P('gx', 'gy'), may hold values from 0 to 576, as said below
- counts: int32 [16, 8], P(None, 'gy'), may hold values from 769 to 2048, as said below
- neighbours: int32 [16, 8, 16, 4], P('gx', 'gy'), may hold values from 0 to 143, as said below
- w_query: bfloat16 [128, 128], replicated, may hold values from -0.5 to 0.5
- w_key: bfloat16 [128, 128], replicated, may hold values from -0.5 to 0.5
- w_value: bfloat16 [128, 128], replicated, may hold values from -0.5 to 0.5
- w_radial: bfloat16 [16, 64], replicated, may hold values from -1.5 to 1.5
- b_radial: float32 [64], replicated, may hold values from -4 to 4
- w_head: bfloat16 [64, 8], replicated, may hold values from -0.75 to 0.75
Outputs:
- messages: bfloat16 [16, 8, 2048, 128], P('gx', 'gy')
Inputs may be any that keep to these rules, and one draw needn't show every extreme that they name: `counts`: in every line of bricks along the first box axis exactly one brick holds min(16, 23) * 128 atoms; every other holds more than max(6, 0) * 128 and at most (7) * 128. `positions`: the first two coordinates lie in 0 to 6. Along the third, all bricks span the same length, 576: live slot s of a brick with c live atoms lies between s and s + 1 times that length over c. `neighbours`: entry 0 of query block q is the block itself, 64 + q; the other entries are live blocks of distinct bricks of the neighbourhood other than the centre.
All inputs are finite; a program needn't handle non-finite values.
Results may differ from a plain program's by a relative error of at most 0.012.
Values may be sent and summed in bfloat16 or wider, within the bound.
No kernel may reach another device: no remote copies, remote signals or barrier semaphores. Data moves between devices by JAX's collectives and lax.ppermute only.
A program may use at most 128 MiB of HBM per device.

v0:
```python
import math

import jax
import jax.numpy as jnp
from jax import lax
from jax.experimental import pallas as pl
from jax.experimental.pallas import tpu as pltpu
from jax.sharding import PartitionSpec as P

HEADS = 8
ATOM_BLOCK = 128
KEY_BLOCKS = 4
CUTOFF = 6.0
SHARPNESS = 4.0
MASKED = -1e30
LENGTH = 576.0
FAR = float(2**20)
POS_ROWS = 16
ROWS = ATOM_BLOCK + POS_ROWS
CHUNK = 8
LIGHT_BLOCKS = 7
UNITS = 32
SOURCES = 6


def payload_kernel(scalars_ref, rows_ref, pos_ref, light_ref, extra_ref):
    f32 = jnp.float32
    bf16 = jnp.bfloat16
    count = scalars_ref[0]
    lane = lax.broadcasted_iota(jnp.int32, (1, ATOM_BLOCK), 1)
    high_count = jnp.broadcast_to((count // 16 * 16).astype(f32), (1, ATOM_BLOCK))
    low_count = jnp.broadcast_to((count % 16).astype(f32), (1, ATOM_BLOCK))
    zeros = jnp.zeros((2, ATOM_BLOCK), f32)
    for q in range(rows_ref.shape[0] // ATOM_BLOCK):
        light = q < LIGHT_BLOCKS
        out = light_ref.at[q] if light else extra_ref.at[q - LIGHT_BLOCKS]
        at = slice(q * ATOM_BLOCK, (q + 1) * ATOM_BLOCK)
        out[:ATOM_BLOCK, :] = rows_ref[at, :]
        pos = pos_ref[:, at]
        pos = jnp.concatenate(
            [pos[:2], jnp.where(lane + q * ATOM_BLOCK < count, pos[2:3], FAR)], 0
        )
        hi = pos.astype(bf16).astype(f32)
        rest = pos - hi
        mid = rest.astype(bf16).astype(f32)
        begin = jnp.full((1, ATOM_BLOCK), float(q * ATOM_BLOCK), f32)
        terms = [hi, mid, rest - mid, zeros, high_count, low_count, begin, zeros]
        out[ATOM_BLOCK:, :] = jnp.concatenate(terms, 0).astype(bf16)


def make_payload(scalars, rows, pos):
    blocks = rows.shape[0] // ATOM_BLOCK
    return pl.pallas_call(
        payload_kernel,
        out_shape=[
            jax.ShapeDtypeStruct((n, ROWS, rows.shape[1]), jnp.bfloat16)
            for n in (LIGHT_BLOCKS, blocks - LIGHT_BLOCKS)
        ],
        in_specs=[pl.BlockSpec(memory_space=pltpu.SMEM)]
        + [pl.BlockSpec(memory_space=pltpu.VMEM)] * 2,
        out_specs=[pl.BlockSpec(memory_space=pltpu.VMEM)] * 2,
        name="payload",
    )(scalars, rows, pos)


def weights_kernel(key_ref, value_ref, radial_ref, bias_ref, head_ref, kv_ref, w1_ref, b1_ref, w2_ref):
    f32 = jnp.float32
    bf16 = jnp.bfloat16

    def split(shape, axis):
        index = lax.broadcasted_iota(jnp.int32, shape, axis)
        return lax.shift_right_logical(index, 3), index & (CHUNK - 1)

    def pick(condition):
        return jnp.where(condition, 1.0, 0.0).astype(bf16)

    def index(shape, axis):
        return lax.broadcasted_iota(jnp.int32, shape, axis)

    basis, radial = radial_ref.shape
    width, tall, heads = basis * CHUNK, radial * CHUNK, HEADS * CHUNK
    kv_ref[:, : key_ref.shape[1]] = key_ref[...]
    kv_ref[:, key_ref.shape[1] :] = value_ref[...]
    first = (((0,), (0,)), ((), ()))
    spread = pick(split((basis, width), 1)[0] == index((basis, width), 0))
    w1 = lax.dot_general(radial_ref[...], spread, first, preferred_element_type=f32)
    rows = pick(split((tall, radial), 0)[0] == index((tall, radial), 1))
    w1 = jnp.dot(rows, w1.astype(bf16), preferred_element_type=f32)
    same = split((tall, width), 0)[1] == split((tall, width), 1)[1]
    w1_ref[...] = jnp.where(same, 0.5 * w1, 0.0).astype(bf16)
    spread = pick(split((radial, tall), 1)[0] == index((radial, tall), 0))
    w2 = lax.dot_general(head_ref[...], spread, first, preferred_element_type=f32)
    rows = pick(split((heads, HEADS), 0)[0] == index((heads, HEADS), 1))
    w2 = jnp.dot(rows, w2.astype(bf16), preferred_element_type=f32)
    same = split((heads, tall), 0)[1] == split((heads, tall), 1)[1]
    w2_ref[...] = jnp.where(same, w2, 0.0).astype(bf16)
    here = split((tall, radial), 0)[0] == index((tall, radial), 1)
    bias = jnp.sum(jnp.where(here, 0.5 * bias_ref[...], 0.0), axis=1, keepdims=True)
    b1_ref[...] = jnp.broadcast_to(bias, b1_ref.shape)


def make_weights(w_key, w_value, w_radial, b_radial, w_head):
    basis, radial = w_radial.shape
    channels = w_key.shape[0]
    bf16 = jnp.bfloat16
    return pl.pallas_call(
        weights_kernel,
        out_shape=[
            jax.ShapeDtypeStruct((channels, 2 * channels), bf16),
            jax.ShapeDtypeStruct((radial * CHUNK, basis * CHUNK), bf16),
            jax.ShapeDtypeStruct((radial * CHUNK, 128), jnp.float32),
            jax.ShapeDtypeStruct((HEADS * CHUNK, radial * CHUNK), bf16),
        ],
        in_specs=[pl.BlockSpec(memory_space=pltpu.VMEM)] * 5,
        out_specs=[pl.BlockSpec(memory_space=pltpu.VMEM)] * 4,
        name="weights",
    )(w_key, w_value, w_radial, b_radial[None], w_head)


def attend_kernel(info_ref, lists_ref, *refs):
    srcs = refs[:SOURCES]
    wq_ref, wkv_ref, w1_ref, b1_ref, w2_ref, out_ref = refs[SOURCES : SOURCES + 6]
    xbuf, sems, kvp_s, q_s, qp_s, acc_s, basis_s, active_s, logit_s, coef_s, den_s, v_s, r2_s, env_s, table_v, table_sem, items_ref, order_ref = refs[SOURCES + 6 :]
    blocks = out_ref.shape[0] // ATOM_BLOCK
    slots = blocks * ATOM_BLOCK
    dummy = blocks * KEY_BLOCKS * ATOM_BLOCK
    count = info_ref[0]
    chunks = ATOM_BLOCK // CHUNK
    none = blocks * chunks
    live_blocks = (count + ATOM_BLOCK - 1) // ATOM_BLOCK
    bf16 = jnp.bfloat16
    f32 = jnp.float32

    def listed(q, e):
        item = lists_ref[q, e]
        brick = lax.shift_right_logical(item, 4)
        part = lax.shift_right_logical(brick * 11, 5)
        return item, item & (blocks - 1), part, brick - 3 * part

    def fetch(q, carry):
        for e in range(KEY_BLOCKS):
            _, block, part, side = listed(q, e)
            light = block < LIGHT_BLOCKS
            source = jnp.where(light, part, 3 + side)
            block = jnp.where(light, side * LIGHT_BLOCKS + block, block - LIGHT_BLOCKS)

            def among(low, high):
                if high - low == 1:
                    pltpu.make_async_copy(
                        srcs[low].at[block], xbuf.at[q, e], sems.at[q, e]
                    ).start()
                    return
                middle = (low + high) // 2
                pl.when(source < middle)(lambda: among(low, middle))
                pl.when(source >= middle)(lambda: among(middle, high))

            among(0, SOURCES)
        return carry

    lax.fori_loop(0, live_blocks, fetch, 0)

    lane = lax.broadcasted_iota(jnp.int32, (CHUNK, 128), 1)
    head_of = lane // 16
    sub2 = lax.broadcasted_iota(jnp.int32, (2 * CHUNK, 128), 0)
    lane2 = lax.broadcasted_iota(jnp.int32, (2 * CHUNK, 128), 1)
    head_masks = [
        jnp.where(lane2 // 16 == 2 * i + sub2 // CHUNK, 1.0, 0.0).astype(bf16) for i in range(4)
    ]

    kvp_s[0, pl.ds(dummy, 8), :] = jnp.zeros((8, 128), f32)
    kvp_s[1, pl.ds(dummy, 8), :] = jnp.zeros((8, 128), f32)
    kvp_s[2, pl.ds(dummy, 8), :] = jnp.where(
        lane % 64 == 2, FAR, 0.0
    ).astype(f32)
    q_s[pl.ds(slots, 8), :] = jnp.zeros((8, 128), f32)
    qp_s[pl.ds(slots, 8), :] = jnp.zeros((8, 128), f32)
    for ref in (basis_s, active_s, logit_s, coef_s, den_s, v_s, r2_s, env_s):
        ref[...] = jnp.zeros_like(ref)

    def project(q, carry):
        for e in range(KEY_BLOCKS):
            pltpu.make_async_copy(srcs[0].at[0], xbuf.at[q, e], sems.at[q, e]).wait()

        unit = lax.broadcasted_iota(jnp.int32, (chunks, 128), 1).astype(f32)
        chunk_id = lax.broadcasted_iota(jnp.int32, (chunks, 128), 0)
        first = (q * ATOM_BLOCK + CHUNK * chunk_id).astype(f32)
        rows = jnp.full((chunks, 128), float(dummy), f32)
        ends = jnp.zeros((chunks, 128), f32)
        mats = []
        for e in range(KEY_BLOCKS):
            _, _, part, side = listed(q, e)
            shift_x = (part - 1).astype(f32) * CUTOFF
            shift_y = (side - 1).astype(f32) * CUTOFF
            m = xbuf[q, e, ATOM_BLOCK:, :].astype(f32)
            key_count = m[11:12] + m[12:13]
            ratio = key_count / count.astype(f32)
            reach = key_count * (CUTOFF / LENGTH)
            begin = m[13:14]
            low = jnp.floor(first * ratio - reach - 1.05) + 1.0 - begin
            high = jnp.ceil((first + CHUNK) * ratio + reach + 0.05) - 1.0 - begin
            low = jnp.maximum(low, 0.0)
            high = jnp.minimum(high, jnp.minimum(key_count - 1.0 - begin, ATOM_BLOCK - 1.0))
            size = jnp.where(first < count.astype(f32), jnp.maximum(high - low + 1.0, 0.0), 0.0)
            units = jnp.floor((size + 7.0) * 0.125)
            low = jnp.minimum(low, ATOM_BLOCK - 8.0 * units)
            base = ((q * KEY_BLOCKS + e) * ATOM_BLOCK).astype(f32)
            rows = jnp.where(
                (unit >= ends) & (unit < ends + units), base + low + 8.0 * (unit - ends), rows
            )
            ends = ends + units
            place = (m[0:3] + m[3:6]) + m[6:9]
            axis = lax.broadcasted_iota(jnp.int32, (3, 128), 0)
            place = place + jnp.where(axis == 0, shift_x, jnp.where(axis == 1, shift_y, 0.0))
            mats.append(jnp.concatenate([place, jnp.zeros((13, 128), f32)], 0))
        turned = jnp.transpose(jnp.concatenate(mats + mats, 0))
        own = pl.ds(pl.multiple_of(q * ATOM_BLOCK, ATOM_BLOCK), ATOM_BLOCK)
        qp_s[own, :] = turned
        for e in range(KEY_BLOCKS):
            at = pl.ds(
                pl.multiple_of((q * KEY_BLOCKS + e) * ATOM_BLOCK, ATOM_BLOCK), ATOM_BLOCK
            )
            kvp_s[2, at, :] = pltpu.roll(turned, 128 - 16 * e, 1) if e else turned
            x = xbuf[q, e, :ATOM_BLOCK, :]
            kv = jnp.dot(x, wkv_ref[...], preferred_element_type=f32)
            kv = kv.astype(bf16).astype(f32)
            kvp_s[0, at, :] = kv[:, :128]
            kvp_s[1, at, :] = kv[:, 128:]
        query = jnp.dot(xbuf[q, 0, :ATOM_BLOCK, :], wq_ref[...], preferred_element_type=f32)
        q_s[own, :] = query.astype(bf16).astype(f32) * 0.25
        wide = jnp.where(ends > UNITS // 2, 1.0, 0.0)
        even = chunk_id % 2 == 0
        wide = jnp.maximum(
            wide, jnp.where(even, pltpu.roll(wide, chunks - 1, 0), pltpu.roll(wide, 1, 0))
        )
        following = pltpu.roll(pltpu.roll(rows, chunks - 1, 0), UNITS // 2, 1)
        joined = (wide < 0.5) & (unit >= UNITS // 2)
        rows = jnp.where(joined, following, rows)
        rows = jnp.where(unit == UNITS, wide, rows)
        at = pl.ds(pl.multiple_of(q * chunks, chunks), chunks)
        table_v[at, :] = rows.astype(jnp.int32)
        pltpu.make_async_copy(table_v.at[at], items_ref.at[at], table_sem.at[q]).start()
        return carry

    end = pl.ds(none, 8)
    table_v[end, :] = jnp.where(lane == UNITS, 0, dummy)
    last = pltpu.make_async_copy(table_v.at[end], items_ref.at[end], table_sem.at[blocks])
    last.start()
    lax.fori_loop(0, live_blocks, project, 0)
    last.wait()

    def await_table(q, carry):
        at = pl.ds(pl.multiple_of(q * chunks, chunks), chunks)
        pltpu.make_async_copy(table_v.at[at], items_ref.at[at], table_sem.at[q]).wait()
        return carry

    lax.fori_loop(0, live_blocks, await_table, 0)

    def enlist(p, n):
        order_ref[n] = 2 * p
        order_ref[n + 1] = 2 * p + 1
        return n + 1 + items_ref[2 * p, UNITS]

    for n in range(4):
        order_ref[n] = none
    total = lax.fori_loop(
        0, lax.shift_right_logical(count + 2 * CHUNK - 1, 4), enlist, 4
    )
    for n in range(4):
        order_ref[total + n] = none

    contract_last = (((1,), (1,)), ((), ()))
    top_half = w1_ref.shape[0] // 2

    def query_rows(item):
        pair = lax.shift_right_logical(item, 1)
        wide = items_ref[item, UNITS]
        first = jnp.where(wide != 0, item, 2 * pair)
        second = jnp.where(wide != 0, item, 2 * pair + 1)
        first = jnp.minimum(first * CHUNK, slots)
        second = jnp.minimum(second * CHUNK, slots)
        return wide, (pl.multiple_of(first, CHUNK), pl.multiple_of(second, CHUNK))


    def stage_a(item, slot):
        _, starts = query_rows(item)
        places = []
        for half in range(2):
            at = slice(128 * half, 128 * (half + 1))
            parts = [[], [], []]
            for j in range(UNITS // 2):
                row = items_ref[item, half * (UNITS // 2) + j]
                for n in range(3):
                    parts[n].append(kvp_s[n, pl.ds(row, 8), :])
            places.append(parts[2])
            keys = jnp.concatenate(parts[0], 0).astype(bf16)
            v_s[pl.ds(pl.multiple_of((slot & 7) * 256 + 128 * half, 128), 128), :] = (
                jnp.concatenate(parts[1], 0).astype(bf16)
            )
            qc = q_s[pl.ds(starts[half], CHUNK), :]
            qq = jnp.concatenate([qc, qc], 0).astype(bf16)
            q_exp = jnp.concatenate([qq * m for m in head_masks], 0)
            logit_s[pl.ds(pl.multiple_of((slot & 3) * 64, 64), 64), at] = lax.dot_general(
                q_exp, keys, contract_last, preferred_element_type=f32
            )
            yield
        turned = jnp.transpose(
            jnp.concatenate([jnp.where(lane < 64, x, y) for x, y in zip(*places)], 0)
        )
        yield
        for half in range(2):
            at = slice(128 * half, 128 * (half + 1))
            qp = qp_s[pl.ds(starts[half], CHUNK), :]
            r2 = 0.0
            for a in range(3):
                diff = qp[:, a : a + 1] - turned[64 * half + a : 64 * half + a + 1, :]
                r2 = r2 + diff * diff
            r2_s[:, at] = r2
            yield

    def stage_g(r2_both, slot):
        scale = math.sqrt(SHARPNESS * math.log2(math.e))
        for half in range(2):
            at = slice(128 * half, 128 * (half + 1))
            r2 = r2_both[:, at]
            valid = r2 < CUTOFF * CUTOFF
            inside = 1.0 - r2 * (1.0 / (CUTOFF * CUTOFF))
            env_s[pl.ds(pl.multiple_of((slot & 3) * 8, 8), 8), at] = jnp.where(
                valid, 2.0 * jnp.log(jnp.where(valid, inside, 1.0)), MASKED
            )
            r = jnp.sqrt(r2) * scale
            yield
            for k in range(0, 16, 2):
                two = []
                for kk in (k, k + 1):
                    t = r - (CUTOFF / 15 * kk) * scale
                    two.append(jnp.exp2(-(t * t)))
                basis_s[8 * k : 8 * k + 16, at] = jnp.concatenate(two, 0).astype(bf16)
                yield

    def stage_b(hidden, base):
        for t in range(0, hidden.shape[0], 16):
            bias = b1_ref[base + t : base + t + 16, :]
            x = hidden[t : t + 16] + jnp.concatenate([bias, bias], 1)
            active_s[base + t : base + t + 16, :] = (x + x * jnp.tanh(x)).astype(bf16)
            yield

    def stage_c(item, logits, env, expos):
        wide, _ = query_rows(item)
        dens = [[], []]
        for h in range(HEADS):
            rows = [
                logits[8 * h : 8 * h + 8, 128 * i : 128 * i + 128] + env[:, 128 * i : 128 * i + 128]
                for i in range(2)
            ]
            tops = [jnp.max(row, axis=1, keepdims=True) for row in rows]
            both = jnp.maximum(tops[0], tops[1])
            yield
            for i in range(2):
                top = jnp.where(wide != 0, both, tops[i])
                expo = jnp.exp(rows[i] - top)
                expos[i].append(expo)
                dens[i].append(jnp.sum(expo, axis=1, keepdims=True))
            yield
        for i in range(2):
            den = jnp.broadcast_to(dens[i][0], (8, 128))
            for h in range(1, HEADS):
                den = jnp.where(head_of == h, dens[i][h], den)
            den_s[:, 128 * i : 128 * (i + 1)] = den
            yield

    def stage_e(expos, filt):
        for h in range(0, HEADS, 2):
            for i in range(2):
                at = slice(128 * i, 128 * (i + 1))
                two = [expos[i][h + n] * filt[8 * (h + n) : 8 * (h + n) + 8, at] for n in range(2)]
                coef_s[8 * h : 8 * h + 16, at] = jnp.concatenate(two, 0).astype(bf16)
            yield

    def stage_d(item, nums, dens):
        wide, starts = query_rows(item)
        yield
        yield
        yield
        res = []
        for i in range(2):
            one = nums[i][0:8]
            for h in range(1, HEADS):
                one = jnp.where(head_of == h, nums[i][8 * h : 8 * h + 8], one)
            res.append(one)
            yield
        for i in range(2):
            num = jnp.where(wide != 0, res[0] + res[1], res[i])
            den = jnp.where(wide != 0, dens[0] + dens[1], dens[i])
            acc_s[pl.ds(starts[i], CHUNK), :] = num / jnp.maximum(den, 1.0)
            yield

    def in_turns(*turns):
        turns = list(turns)
        while turns:
            for turn in list(turns):
                if next(turn, turns) is turns:
                    turns.remove(turn)

    def step(i, carry):
        basis = basis_s[...]
        r2 = r2_s[...]
        logits = logit_s[pl.ds(pl.multiple_of(((i + 1) & 3) * 64, 64), 64), :]
        env = env_s[pl.ds(pl.multiple_of(((i + 1) & 3) * 8, 8), 8), :]
        coef = coef_s[...]
        dens = [den_s[:, 128 * n : 128 * (n + 1)] for n in range(2)]
        active = active_s[...]
        at_v = pl.multiple_of((i & 7) * 256, 256)
        values = [v_s[pl.ds(at_v + 128 * n, 128), :] for n in range(2)]
        filt = [
            jnp.dot(
                w2_ref[:, top_half * n : top_half * (n + 1)],
                active[top_half * n : top_half * (n + 1)],
                preferred_element_type=f32,
            )
            for n in range(2)
        ]
        filt = filt[0] + filt[1]
        nums = [
            jnp.dot(coef[:, 128 * n : 128 * (n + 1)], values[n], preferred_element_type=f32)
            for n in range(2)
        ]
        first = jnp.dot(w1_ref[:top_half], basis, preferred_element_type=f32)
        second = jnp.dot(w1_ref[top_half:], basis, preferred_element_type=f32)
        expos = [[], []]
        in_turns(stage_c(order_ref[i + 1], logits, env, expos), stage_d(order_ref[i], nums, dens), stage_g(r2, i + 3))
        in_turns(stage_b(first, 0), stage_b(second, top_half), stage_a(order_ref[i + 4], i + 4), stage_e(expos, filt))
        return carry

    lax.fori_loop(0, total, step, 0)

    def finish(q, carry):
        at = pl.ds(pl.multiple_of(q * ATOM_BLOCK, ATOM_BLOCK), ATOM_BLOCK)
        row_id = lax.broadcasted_iota(jnp.int32, (ATOM_BLOCK, 128), 0) + q * ATOM_BLOCK
        out_ref[at, :] = jnp.where(row_id < count, acc_s[at, :], 0.0).astype(bf16)
        return carry

    lax.fori_loop(0, blocks, finish, 0)


def attend(scalars, lists, srcs, wq, wkv, w1, b1, w2):
    blocks = lists.shape[0]
    channels = srcs[0].shape[2]
    smem = pl.BlockSpec(memory_space=pltpu.SMEM)
    vmem = pl.BlockSpec(memory_space=pltpu.VMEM)
    hbm = pl.BlockSpec(memory_space=pl.ANY)
    f32 = jnp.float32
    slots = blocks * ATOM_BLOCK
    table = (slots // CHUNK + 8, 128)
    return pl.pallas_call(
        attend_kernel,
        out_shape=jax.ShapeDtypeStruct((slots, channels), jnp.bfloat16),
        in_specs=[smem] * 2 + [hbm] * SOURCES + [vmem] * 5,
        out_specs=vmem,
        scratch_shapes=[
            pltpu.VMEM((blocks, KEY_BLOCKS, ROWS, channels), jnp.bfloat16),
            pltpu.SemaphoreType.DMA((blocks, KEY_BLOCKS)),
            pltpu.VMEM((3, slots * KEY_BLOCKS + 8, 128), f32),
            pltpu.VMEM((slots + 8, 128), f32),
            pltpu.VMEM((slots + 8, 128), f32),
            pltpu.VMEM((slots + 8, 128), f32),
            pltpu.VMEM((128, 256), jnp.bfloat16),
            pltpu.VMEM((512, 256), jnp.bfloat16),
            pltpu.VMEM((256, 256), f32),
            pltpu.VMEM((64, 256), jnp.bfloat16),
            pltpu.VMEM((8, 256), f32),
            pltpu.VMEM((2048, 128), jnp.bfloat16),
            pltpu.VMEM((8, 256), f32),
            pltpu.VMEM((32, 256), f32),
            pltpu.VMEM(table, jnp.int32),
            pltpu.SemaphoreType.DMA((blocks + 1,)),
            pltpu.SMEM(table, jnp.int32),
            pltpu.SMEM((slots // CHUNK + 8,), jnp.int32),
        ],
        name="attend",
    )(scalars, lists, *srcs, wq, wkv, w1, b1, w2)


def shift(x, axis, by):
    size = lax.axis_size(axis)
    return lax.ppermute(x, axis, [(i, (i + by) % size) for i in range(size)])


def shards(
    features, positions, counts, neighbours, w_query, w_key, w_value, w_radial, b_radial, w_head
):
    row = lax.axis_index("gx")
    rows = lax.axis_size("gx")
    line = counts[:, 0]
    scalars = line[row][None]
    light, extra = make_payload(scalars, features[0, 0], positions[0, 0])
    dense = line > LIGHT_BLOCKS * ATOM_BLOCK
    extra = jnp.where(
        dense[(row - 1) % rows],
        shift(extra, "gx", 1),
        jnp.where(dense[(row + 1) % rows], shift(extra, "gx", -1), extra),
    )
    low, high = shift(light, "gy", 1), shift(light, "gy", -1)
    further = [shift(extra, "gy", 1), extra, shift(extra, "gy", -1)]
    low, high, _ = lax.optimization_barrier((low, high, extra))
    column = jnp.concatenate([low, light, high], 0)
    srcs = [shift(column, "gx", 1), column, shift(column, "gx", -1)] + further
    wkv, w1, b1, w2 = make_weights(w_key, w_value, w_radial, b_radial, w_head)
    out = attend(scalars, neighbours[0, 0], srcs, w_query, wkv, w1, b1, w2)
    return out[None, None]


def solution(mesh):
    in_specs = (
        P("gx", "gy", None, None),
        P("gx", "gy", None, None),
        P(None, "gy"),
        P("gx", "gy", None, None),
        P(), P(), P(), P(), P(), P(),
    )
    out_specs = P("gx", "gy", None, None)
    return jax.shard_map(shards, mesh=mesh, in_specs=in_specs, out_specs=out_specs, check_vma=False)
```

profile of v0, /device:TPU:118, one launch (start us, length us, event | category | flops | bytes accessed | tf_op | source)
XLA Modules:
  0.0 117.1 jit_solution(11385590856750473341)
XLA Ops:
  0.0 1.4 %copy.15 = f32[1,1,3,2048]{3,2,1,0:T(4,128)} copy(f32[1,1,3,2048]{3,1,2,0:T(1,128)} %param.11) | data formatting | bytes 49152
  1.4 0.7 copy-done.9
  2.0 0.6 constant_dynamic-slice_fusion.2
  2.7 2.6 %payload.1 = (bf16[7,144,128]{2,1,0:T(8,128)(2,1)}, bf16[9,144,128]{2,1,0:T(8,128)(2,1)}) custom-call(s32[1]{0:T(128)} %bitcast.scalars_ref.info_ref, bf16[2048,128]{1,0:T(8,128)(2,1)} %bitcast.10, f32[3,2048]{1,0:T(4,128)} %bitcast.11), custom_call_target="tpu_custom_call" | custom-call | tf_op jit(solution)/shard_map/payload/pallas_call | solution.py:53
  5.2 0.0 collective-permute-start.3
  5.2 0.5 collective-permute-start.2
  5.8 1.4 %collective-permute-start.1 = (bf16[7,144,128]{2,1,0:T(8,128)(2,1)}, bf16[7,144,128]{2,1,0:T(8,128)(2,1)S(1)}, u32[]{:S(2)}, u32[]{:S(2)}) collective-permute-start(bf16[7,144,128]{2,1,0:T(8,128)(2,1)} %get-tuple-element.13), channel_id=1, source_target_pairs={{0,7},{1,0},{2,1},{3,2},{4,3},{5,4},{6,5},{7,6},{8,15},{9,8},{10,9... | collective-permute-start | bytes 774152 | tf_op jit(solution)/shard_map/ppermute | solution.py:485
  7.2 3.0 %collective-permute-start = (bf16[7,144,128]{2,1,0:T(8,128)(2,1)}, bf16[7,144,128]{2,1,0:T(8,128)(2,1)S(1)}, u32[]{:S(2)}, u32[]{:S(2)}) collective-permute-start(bf16[7,144,128]{2,1,0:T(8,128)(2,1)} %get-tuple-element.13), channel_id=1, source_target_pairs={{0,1},{1,2},{2,3},{3,4},{4,5},{5,6},{6,7},{7,0},{8,9},{9,10},{10,1... | collective-permute-start | bytes 774152 | tf_op jit(solution)/shard_map/ppermute | solution.py:485
  10.2 0.7 constant_dynamic-slice_fusion.1
  10.8 0.0 collective-permute-done.3
  10.8 1.2 collective-permute-done.2
  12.0 2.4 %select_select_fusion.refs_4_ = bf16[9,144,128]{2,1,0:T(8,128)(2,1)S(1)} fusion(bf16[9,144,128]{2,1,0:T(8,128)(2,1)S(1)} %collective-permute-done.2, bf16[9,144,128]{2,1,0:T(8,128)(2,1)S(1)} %collective-permute-done.3, bf16[9,144,128]{2,1,0:T(8,128)(2,1)} %get-tuple-element.14, pred[]{:T(512)} %bitcast.4, pred[]{:T(512)} %bitcast.3), kind=kLoop, calls=%fused_computation | loop fusion | flops 331776 | bytes 1327106 | tf_op jit(solution)/shard_map/jit(_where)/select_n | solution.py:497
  14.4 0.0 copy-start.6
  14.4 2.8 %collective-permute-done.1 = bf16[7,144,128]{2,1,0:T(8,128)(2,1)S(1)} collective-permute-done((bf16[7,144,128]{2,1,0:T(8,128)(2,1)}, bf16[7,144,128]{2,1,0:T(8,128)(2,1)S(1)}, u32[]{:S(2)}, u32[]{:S(2)}) %collective-permute-start.1) | collective-permute-done | bytes 258080 | tf_op jit(solution)/shard_map/ppermute | solution.py:485
  17.3 4.2 %collective-permute-done = bf16[7,144,128]{2,1,0:T(8,128)(2,1)S(1)} collective-permute-done((bf16[7,144,128]{2,1,0:T(8,128)(2,1)}, bf16[7,144,128]{2,1,0:T(8,128)(2,1)S(1)}, u32[]{:S(2)}, u32[]{:S(2)}) %collective-permute-start) | collective-permute-done | bytes 258080 | tf_op jit(solution)/shard_map/ppermute | solution.py:485
  21.6 0.0 copy-start.7
  21.6 0.4 collective-permute-start.5
  22.0 3.6 %collective-permute-start.4 = (bf16[21,144,128]{2,1,0:T(8,128)(2,1)S(1)}, bf16[21,144,128]{2,1,0:T(8,128)(2,1)S(1)}, u32[]{:S(2)}, u32[]{:S(2)}) collective-permute-start(bf16[21,144,128]{2,1,0:T(8,128)(2,1)S(1)} %constant_dynamic-update-slice_fusion.refs_1_), channel_id=1, source_target_pairs={{0,8},{8,16},{16,24},{24,32},{32,40},{40,48},{48,56},{56,64},{64,7... | collective-permute-start | bytes 2322440 | tf_op jit(solution)/shard_map/ppermute | solution.py:485
  25.6 1.4 %collective-permute-start.7 = (bf16[9,144,128]{2,1,0:T(8,128)(2,1)S(1)}, bf16[9,144,128]{2,1,0:T(8,128)(2,1)S(1)}, u32[]{:S(2)}, u32[]{:S(2)}) collective-permute-start(bf16[9,144,128]{2,1,0:T(8,128)(2,1)S(1)} %select_select_fusion.refs_4_), channel_id=1, source_target_pairs={{0,7},{1,0},{2,1},{3,2},{4,3},{5,4},{6,5},{7,6},{8,15},{9,8},{10,9... | collective-permute-start | bytes 995336 | tf_op jit(solution)/shard_map/ppermute | solution.py:485
  27.1 3.0 %collective-permute-start.6 = (bf16[9,144,128]{2,1,0:T(8,128)(2,1)S(1)}, bf16[9,144,128]{2,1,0:T(8,128)(2,1)S(1)}, u32[]{:S(2)}, u32[]{:S(2)}) collective-permute-start(bf16[9,144,128]{2,1,0:T(8,128)(2,1)S(1)} %select_select_fusion.refs_4_), channel_id=1, source_target_pairs={{0,1},{1,2},{2,3},{3,4},{4,5},{5,6},{6,7},{7,0},{8,9},{9,10},{10,1... | collective-permute-start | bytes 995336 | tf_op jit(solution)/shard_map/ppermute | solution.py:485
  30.1 0.7 copy.12.lists_ref
  30.8 0.0 copy-done.8
  30.8 0.7 copy.11.head_ref
  31.5 2.0 %weights.1 = (bf16[128,256]{1,0:T(8,128)(2,1)}, bf16[512,128]{1,0:T(8,128)(2,1)}, f32[512,128]{1,0:T(8,128)}, bf16[64,512]{1,0:T(8,128)(2,1)}) custom-call(bf16[128,128]{1,0:T(8,128)(2,1)} %key_ref.1, bf16[128,128]{1,0:T(8,128)(2,1)} %value_ref.1, bf16[16,64]{1,0:T(8,128)(2,1)} %radial_ref.1, f32[1,64]{1,0:T(1,128)} %bitcast.13, bf16[64,8]{1,0:T(8,128)(2,1)} %copy.11.head_ref), custom_call_target="tpu_custom_call" | custom-call | tf_op jit(solution)/shard_map/weights/pallas_call | solution.py:106
  33.4 4.2 %collective-permute-done.7.refs_5_ = bf16[9,144,128]{2,1,0:T(8,128)(2,1)S(1)} collective-permute-done((bf16[9,144,128]{2,1,0:T(8,128)(2,1)S(1)}, bf16[9,144,128]{2,1,0:T(8,128)(2,1)S(1)}, u32[]{:S(2)}, u32[]{:S(2)}) %collective-permute-start.7) | collective-permute-done | bytes 331808 | tf_op jit(solution)/shard_map/ppermute | solution.py:485
  37.6 6.1 %collective-permute-done.6.refs_3_ = bf16[9,144,128]{2,1,0:T(8,128)(2,1)S(1)} collective-permute-done((bf16[9,144,128]{2,1,0:T(8,128)(2,1)S(1)}, bf16[9,144,128]{2,1,0:T(8,128)(2,1)S(1)}, u32[]{:S(2)}, u32[]{:S(2)}) %collective-permute-start.6) | collective-permute-done | bytes 331808 | tf_op jit(solution)/shard_map/ppermute | solution.py:485
  43.7 0.0 collective-permute-done.5.refs_2_
  43.8 0.0 collective-permute-done.4.refs_0_
  43.8 0.7 copy-done.5
  44.5 0.2 copy-done.2
  44.7 0.2 copy-done.3
  45.0 72.1 %attend.1 = bf16[2048,128]{1,0:T(8,128)(2,1)} custom-call(s32[1]{0:T(128)} %bitcast.scalars_ref.info_ref, s32[16,4]{1,0:T(8,128)} %copy.12.lists_ref, bf16[21,144,128]{2,1,0:T(8,128)(2,1)} %copy-done.3, bf16[21,144,128]{2,1,0:T(8,128)(2,1)} %copy-done, bf16[21,144,128]{2,1,0:T(8,128)(2,1)} %copy-done.2, bf16[9,144,128]{2,1,0:T(8,128)(2,1)} %copy-done.5, ...), custom_call_target="tpu_custom_call" | custom-call | tf_op jit(solution)/shard_map/attend/pallas_call | solution.py:454
  (17 shorter events, 0.1 us)
Async XLA Ops:
  1.4 0.7 copy-start.9
  5.2 5.6 %collective-permute-start.3 = (bf16[9,144,128]{2,1,0:T(8,128)(2,1)}, bf16[9,144,128]{2,1,0:T(8,128)(2,1)S(1)}, u32[]{:S(2)}, u32[]{:S(2)}) collective-permute-start(bf16[9,144,128]{2,1,0:T(8,128)(2,1)} %get-tuple-element.14), channel_id=1, source_target_pairs={{0,120},{8,0},{16,8},{24,16},{32,24},{40,32},{48,40},{56,48},{64,5... | collective-permute-start | bytes 995336 | tf_op jit(solution)/shard_map/ppermute | solution.py:485
  5.2 6.8 %collective-permute-start.2 = (bf16[9,144,128]{2,1,0:T(8,128)(2,1)}, bf16[9,144,128]{2,1,0:T(8,128)(2,1)S(1)}, u32[]{:S(2)}, u32[]{:S(2)}) collective-permute-start(bf16[9,144,128]{2,1,0:T(8,128)(2,1)} %get-tuple-element.14), channel_id=1, source_target_pairs={{0,8},{8,16},{16,24},{24,32},{32,40},{40,48},{48,56},{56,64},{64,7... | collective-permute-start | bytes 995336 | tf_op jit(solution)/shard_map/ppermute | solution.py:485
  5.8 11.5 %collective-permute-start.1 = (bf16[7,144,128]{2,1,0:T(8,128)(2,1)}, bf16[7,144,128]{2,1,0:T(8,128)(2,1)S(1)}, u32[]{:S(2)}, u32[]{:S(2)}) collective-permute-start(bf16[7,144,128]{2,1,0:T(8,128)(2,1)} %get-tuple-element.13), channel_id=1, source_target_pairs={{0,7},{1,0},{2,1},{3,2},{4,3},{5,4},{6,5},{7,6},{8,15},{9,8},{10,9... | collective-permute-start | bytes 774152 | tf_op jit(solution)/shard_map/ppermute | solution.py:485
  7.2 14.3 %collective-permute-start = (bf16[7,144,128]{2,1,0:T(8,128)(2,1)}, bf16[7,144,128]{2,1,0:T(8,128)(2,1)S(1)}, u32[]{:S(2)}, u32[]{:S(2)}) collective-permute-start(bf16[7,144,128]{2,1,0:T(8,128)(2,1)} %get-tuple-element.13), channel_id=1, source_target_pairs={{0,1},{1,2},{2,3},{3,4},{4,5},{5,6},{6,7},{7,0},{8,9},{9,10},{10,1... | collective-permute-start | bytes 774152 | tf_op jit(solution)/shard_map/ppermute | solution.py:485
  14.4 12.6 %copy-start.1 = (bf16[9,144,128]{2,1,0:T(8,128)(2,1)}, bf16[9,144,128]{2,1,0:T(8,128)(2,1)S(1)}, u32[]{:S(2)}) copy-start(bf16[9,144,128]{2,1,0:T(8,128)(2,1)S(1)} %select_select_fusion.refs_4_) | copy-start | bytes 995332
  14.4 7.1 %copy-start.6 = (bf16[7,144,128]{2,1,0:T(8,128)(2,1)S(1)}, bf16[7,144,128]{2,1,0:T(8,128)(2,1)}, u32[]{:S(2)}) copy-start(bf16[7,144,128]{2,1,0:T(8,128)(2,1)} %get-tuple-element.13) | copy-start | bytes 774148
  21.6 8.5 %copy-start.7 = (s32[1,1,16,4]{2,3,1,0:T(4,128)S(1)}, s32[1,1,16,4]{2,3,1,0:T(4,128)}, u32[]{:S(2)}) copy-start(s32[1,1,16,4]{2,3,1,0:T(4,128)} %param.13) | copy-start | bytes 772
  21.6 22.1 %copy-start = (bf16[21,144,128]{2,1,0:T(8,128)(2,1)}, bf16[21,144,128]{2,1,0:T(8,128)(2,1)S(1)}, u32[]{:S(2)}) copy-start(bf16[21,144,128]{2,1,0:T(8,128)(2,1)S(1)} %constant_dynamic-update-slice_fusion.refs_1_) | copy-start | bytes 2322436
  21.6 22.1 %collective-permute-start.5 = (bf16[21,144,128]{2,1,0:T(8,128)(2,1)S(1)}, bf16[21,144,128]{2,1,0:T(8,128)(2,1)S(1)}, u32[]{:S(2)}, u32[]{:S(2)}) collective-permute-start(bf16[21,144,128]{2,1,0:T(8,128)(2,1)S(1)} %constant_dynamic-update-slice_fusion.refs_1_), channel_id=1, source_target_pairs={{0,120},{8,0},{16,8},{24,16},{32,24},{40,32},{48,40},{56,48},{64,5... | collective-permute-start | bytes 2322440 | tf_op jit(solution)/shard_map/ppermute | solution.py:485
  22.0 21.7 %collective-permute-start.4 = (bf16[21,144,128]{2,1,0:T(8,128)(2,1)S(1)}, bf16[21,144,128]{2,1,0:T(8,128)(2,1)S(1)}, u32[]{:S(2)}, u32[]{:S(2)}) collective-permute-start(bf16[21,144,128]{2,1,0:T(8,128)(2,1)S(1)} %constant_dynamic-update-slice_fusion.refs_1_), channel_id=1, source_target_pairs={{0,8},{8,16},{16,24},{24,32},{32,40},{40,48},{48,56},{56,64},{64,7... | collective-permute-start | bytes 2322440 | tf_op jit(solution)/shard_map/ppermute | solution.py:485
  25.6 12.0 %collective-permute-start.7 = (bf16[9,144,128]{2,1,0:T(8,128)(2,1)S(1)}, bf16[9,144,128]{2,1,0:T(8,128)(2,1)S(1)}, u32[]{:S(2)}, u32[]{:S(2)}) collective-permute-start(bf16[9,144,128]{2,1,0:T(8,128)(2,1)S(1)} %select_select_fusion.refs_4_), channel_id=1, source_target_pairs={{0,7},{1,0},{2,1},{3,2},{4,3},{5,4},{6,5},{7,6},{8,15},{9,8},{10,9... | collective-permute-start | bytes 995336 | tf_op jit(solution)/shard_map/ppermute | solution.py:485
  27.1 16.7 %collective-permute-start.6 = (bf16[9,144,128]{2,1,0:T(8,128)(2,1)S(1)}, bf16[9,144,128]{2,1,0:T(8,128)(2,1)S(1)}, u32[]{:S(2)}, u32[]{:S(2)}) collective-permute-start(bf16[9,144,128]{2,1,0:T(8,128)(2,1)S(1)} %select_select_fusion.refs_4_), channel_id=1, source_target_pairs={{0,1},{1,2},{2,3},{3,4},{4,5},{5,6},{6,7},{7,0},{8,9},{9,10},{10,1... | collective-permute-start | bytes 995336 | tf_op jit(solution)/shard_map/ppermute | solution.py:485
  30.1 0.7 copy-start.8
  37.6 6.1 %copy-start.4 = (bf16[9,144,128]{2,1,0:T(8,128)(2,1)}, bf16[9,144,128]{2,1,0:T(8,128)(2,1)S(1)}, u32[]{:S(2)}) copy-start(bf16[9,144,128]{2,1,0:T(8,128)(2,1)S(1)} %collective-permute-done.7.refs_5_) | copy-start | bytes 995332
  43.7 0.7 copy-start.5
  43.8 1.0 copy-start.2
  43.8 1.2 %copy-start.3 = (bf16[21,144,128]{2,1,0:T(8,128)(2,1)}, bf16[21,144,128]{2,1,0:T(8,128)(2,1)S(1)}, u32[]{:S(2)}) copy-start(bf16[21,144,128]{2,1,0:T(8,128)(2,1)S(1)} %collective-permute-done.4.refs_0_) | copy-start | bytes 2322436
where the time goes:
time: 118 us; the launch traced here: 117 us
  Pallas kernels  76.6 us (65%)
  waiting for transfers between devices  18.5 us (16%)
  starting transfers between devices  13.4 us (11%)
  local copies, waits for them, and re-layouts  6.01 us (5%)
  other arithmetic  2.42 us (2%)
    pallas_call x1, Pallas kernels, attend(): pl.pallas_call(attend_kernel, out_shape=jax.ShapeDtypeStruct((slots, chan...  72.1 us
    ppermute x8, waiting for transfers between devices, shift(): return lax.ppermute(x, axis, [(i, (i + by) % size) for i in range(size)])  18.5 us
    ppermute x8, starting transfers between devices, shift(): return lax.ppermute(x, axis, [(i, (i + by) % size) for i in range(size)])  13.4 us
    unnamed x24, local copies, waits for them, and re-layouts  4 us
    pallas_call x1, Pallas kernels, make_payload(): pl.pallas_call(payload_kernel, out_shape=[jax.ShapeDtypeStruct((n, ROWS,...  2.57 us
    select_n x1, other arithmetic, shards(): jnp.where(dense[(row - 1) % rows], shift(extra, 'gx', 1), jnp.where(dense...  2.41 us
  transfers between devices with their start and end apart: 8, of which 5 were waited for; matrix products, arithmetic and copies ran while one was open for 4% of the time, Pallas kernels for 2%

commit v1 on v0

--- a/solution.py
+++ b/solution.py
@@ -23,10 +23,10 @@
 SOURCES = 6
 
 
-def payload_kernel(scalars_ref, rows_ref, pos_ref, light_ref, extra_ref):
+def payload_kernel(line_ref, row_ref, rows_ref, pos_ref, light_ref, extra_ref):
     f32 = jnp.float32
     bf16 = jnp.bfloat16
-    count = scalars_ref[0]
+    count = line_ref[0, row_ref[0]]
     lane = lax.broadcasted_iota(jnp.int32, (1, ATOM_BLOCK), 1)
     high_count = jnp.broadcast_to((count // 16 * 16).astype(f32), (1, ATOM_BLOCK))
     low_count = jnp.broadcast_to((count % 16).astype(f32), (1, ATOM_BLOCK))
@@ -36,10 +36,9 @@
         out = light_ref.at[q] if light else extra_ref.at[q - LIGHT_BLOCKS]
         at = slice(q * ATOM_BLOCK, (q + 1) * ATOM_BLOCK)
         out[:ATOM_BLOCK, :] = rows_ref[at, :]
-        pos = pos_ref[:, at]
-        pos = jnp.concatenate(
-            [pos[:2], jnp.where(lane + q * ATOM_BLOCK < count, pos[2:3], FAR)], 0
-        )
+        pos = [pos_ref[a, :, at] for a in range(3)]
+        pos[2] = jnp.where(lane + q * ATOM_BLOCK < count, pos[2], FAR)
+        pos = jnp.concatenate(pos, 0)
         hi = pos.astype(bf16).astype(f32)
         rest = pos - hi
         mid = rest.astype(bf16).astype(f32)
@@ -48,7 +47,7 @@
         out[ATOM_BLOCK:, :] = jnp.concatenate(terms, 0).astype(bf16)
 
 
-def make_payload(scalars, rows, pos):
+def make_payload(line, row, rows, pos):
     blocks = rows.shape[0] // ATOM_BLOCK
     return pl.pallas_call(
         payload_kernel,
@@ -56,11 +55,11 @@
             jax.ShapeDtypeStruct((n, ROWS, rows.shape[1]), jnp.bfloat16)
             for n in (LIGHT_BLOCKS, blocks - LIGHT_BLOCKS)
         ],
-        in_specs=[pl.BlockSpec(memory_space=pltpu.SMEM)]
+        in_specs=[pl.BlockSpec(memory_space=pltpu.SMEM)] * 2
         + [pl.BlockSpec(memory_space=pltpu.VMEM)] * 2,
         out_specs=[pl.BlockSpec(memory_space=pltpu.VMEM)] * 2,
         name="payload",
-    )(scalars, rows, pos)
+    )(line, row, rows, pos)
 
 
 def weights_kernel(key_ref, value_ref, radial_ref, bias_ref, head_ref, kv_ref, w1_ref, b1_ref, w2_ref):
@@ -117,14 +116,14 @@
     )(w_key, w_value, w_radial, b_radial[None], w_head)
 
 
-def attend_kernel(info_ref, lists_ref, *refs):
+def attend_kernel(line_ref, row_ref, lists_ref, *refs):
     srcs = refs[:SOURCES]
     wq_ref, wkv_ref, w1_ref, b1_ref, w2_ref, out_ref = refs[SOURCES : SOURCES + 6]
     xbuf, sems, kvp_s, q_s, qp_s, acc_s, basis_s, active_s, logit_s, coef_s, den_s, v_s, r2_s, env_s, table_v, table_sem, items_ref, order_ref = refs[SOURCES + 6 :]
     blocks = out_ref.shape[0] // ATOM_BLOCK
     slots = blocks * ATOM_BLOCK
     dummy = blocks * KEY_BLOCKS * ATOM_BLOCK
-    count = info_ref[0]
+    count = line_ref[0, row_ref[0]]
     chunks = ATOM_BLOCK // CHUNK
     none = blocks * chunks
     live_blocks = (count + ATOM_BLOCK - 1) // ATOM_BLOCK
@@ -154,7 +153,11 @@
                 pl.when(source < middle)(lambda: among(low, middle))
                 pl.when(source >= middle)(lambda: among(middle, high))
 
-            among(0, SOURCES)
+            if e == 0:
+                pl.when(light)(lambda: among(1, 2))
+                pl.when(jnp.logical_not(light))(lambda: among(4, 5))
+            else:
+                among(0, SOURCES)
         return carry
 
     lax.fori_loop(0, live_blocks, fetch, 0)
@@ -442,7 +445,7 @@
     lax.fori_loop(0, blocks, finish, 0)
 
 
-def attend(scalars, lists, srcs, wq, wkv, w1, b1, w2):
+def attend(line, row, lists, srcs, wq, wkv, w1, b1, w2):
     blocks = lists.shape[0]
     channels = srcs[0].shape[2]
     smem = pl.BlockSpec(memory_space=pltpu.SMEM)
@@ -454,7 +457,7 @@
     return pl.pallas_call(
         attend_kernel,
         out_shape=jax.ShapeDtypeStruct((slots, channels), jnp.bfloat16),
-        in_specs=[smem] * 2 + [hbm] * SOURCES + [vmem] * 5,
+        in_specs=[smem] * 3 + [hbm] * SOURCES + [vmem] * 5,
         out_specs=vmem,
         scratch_shapes=[
             pltpu.VMEM((blocks, KEY_BLOCKS, ROWS, channels), jnp.bfloat16),
@@ -477,7 +480,7 @@
             pltpu.SMEM((slots // CHUNK + 8,), jnp.int32),
         ],
         name="attend",
-    )(scalars, lists, *srcs, wq, wkv, w1, b1, w2)
+    )(line, row, lists, *srcs, wq, wkv, w1, b1, w2)
 
 
 def shift(x, axis, by):
@@ -491,8 +494,8 @@
     row = lax.axis_index("gx")
     rows = lax.axis_size("gx")
     line = counts[:, 0]
-    scalars = line[row][None]
-    light, extra = make_payload(scalars, features[0, 0], positions[0, 0])
+    place = (counts.T, row[None])
+    light, extra = make_payload(*place, features[0, 0], positions.transpose(0, 2, 1, 3)[0])
     dense = line > LIGHT_BLOCKS * ATOM_BLOCK
     extra = jnp.where(
         dense[(row - 1) % rows],
@@ -505,7 +508,7 @@
     column = jnp.concatenate([low, light, high], 0)
     srcs = [shift(column, "gx", 1), column, shift(column, "gx", -1)] + further
     wkv, w1, b1, w2 = make_weights(w_key, w_value, w_radial, b_radial, w_head)
-    out = attend(scalars, neighbours[0, 0], srcs, w_query, wkv, w1, b1, w2)
+    out = attend(*place, neighbours[0, 0], srcs, w_query, wkv, w1, b1, w2)
     return out[None, None]
 
 

time: 118 us -> 113 us (0.958)
  local copies, waits for them, and re-layouts: 6.01 us -> 3.99 us
  Pallas kernels: 76.6 us -> 75.1 us
    unnamed x24 -> x23, local copies, waits for them, and re-layouts: 4 us -> 2.63 us
where the time goes in v1:
time: 113 us
  Pallas kernels  75.1 us (66%)
  waiting for transfers between devices  17.9 us (16%)
  starting transfers between devices  13.4 us (12%)
  local copies, waits for them, and re-layouts  3.99 us (4%)
  other arithmetic  2.42 us (2%)
    pallas_call x1, Pallas kernels, attend(): pl.pallas_call(attend_kernel, out_shape=jax.ShapeDtypeStruct((slots, chan...  71.2 us
    ppermute x8, waiting for transfers between devices, shift(): return lax.ppermute(x, axis, [(i, (i + by) % size) for i in range(size)])  17.9 us
    ppermute x8, starting transfers between devices, shift(): return lax.ppermute(x, axis, [(i, (i + by) % size) for i in range(size)])  13.4 us
    unnamed x23, local copies, waits for them, and re-layouts  2.63 us
    select_n x1, other arithmetic, shards(): jnp.where(dense[(row - 1) % rows], shift(extra, 'gx', 1), jnp.where(dense...  2.41 us
  transfers between devices with their start and end apart: 8, of which 5 were waited for; matrix products, arithmetic and copies ran while one was open for 4% of the time, Pallas kernels for 2%

profile of v1, /device:TPU:118, one launch (start us, length us, event | category | flops | bytes accessed | tf_op | source)
XLA Modules:
  0.0 112.9 jit_solution(17454162549542059216)
XLA Ops:
  0.0 1.9 %payload.1 = (bf16[7,144,128]{2,1,0:T(8,128)(2,1)}, bf16[9,144,128]{2,1,0:T(8,128)(2,1)}) custom-call(s32[1,16]{1,0:T(1,128)} %bitcast.12, s32[1]{0:T(128)} %bitcast.1.row_ref, bf16[2048,128]{1,0:T(8,128)(2,1)} %bitcast.9, f32[3,1,2048]{2,1,0:T(1,128)} %bitcast.10), custom_call_target="tpu_custom_call" | custom-call | tf_op jit(solution)/shard_map/payload/pallas_call | solution.py:52
  1.9 0.0 collective-permute-start.3
  1.9 0.5 collective-permute-start.2
  2.4 1.4 %collective-permute-start.1 = (bf16[7,144,128]{2,1,0:T(8,128)(2,1)}, bf16[7,144,128]{2,1,0:T(8,128)(2,1)S(1)}, u32[]{:S(2)}, u32[]{:S(2)}) collective-permute-start(bf16[7,144,128]{2,1,0:T(8,128)(2,1)} %get-tuple-element.13), channel_id=1, source_target_pairs={{0,7},{1,0},{2,1},{3,2},{4,3},{5,4},{6,5},{7,6},{8,15},{9,8},{10,9... | collective-permute-start | bytes 774152 | tf_op jit(solution)/shard_map/ppermute | solution.py:488
  3.8 3.0 %collective-permute-start = (bf16[7,144,128]{2,1,0:T(8,128)(2,1)}, bf16[7,144,128]{2,1,0:T(8,128)(2,1)S(1)}, u32[]{:S(2)}, u32[]{:S(2)}) collective-permute-start(bf16[7,144,128]{2,1,0:T(8,128)(2,1)} %get-tuple-element.13), channel_id=1, source_target_pairs={{0,1},{1,2},{2,3},{3,4},{4,5},{5,6},{6,7},{7,0},{8,9},{9,10},{10,1... | collective-permute-start | bytes 774152 | tf_op jit(solution)/shard_map/ppermute | solution.py:488
  6.8 0.7 copy-done.9
  7.5 0.7 constant_dynamic-slice_fusion.1
  8.2 0.0 collective-permute-done.3
  8.2 0.5 collective-permute-done.2
  8.7 2.4 %select_select_fusion.refs_4_ = bf16[9,144,128]{2,1,0:T(8,128)(2,1)S(1)} fusion(bf16[9,144,128]{2,1,0:T(8,128)(2,1)S(1)} %collective-permute-done.2, bf16[9,144,128]{2,1,0:T(8,128)(2,1)S(1)} %collective-permute-done.3, bf16[9,144,128]{2,1,0:T(8,128)(2,1)} %get-tuple-element.14, pred[]{:T(512)} %bitcast.6, pred[]{:T(512)} %bitcast.5), kind=kLoop, calls=%fused_computation | loop fusion | flops 331776 | bytes 1327106 | tf_op jit(solution)/shard_map/jit(_where)/select_n | solution.py:500
  11.1 0.0 copy-start.6
  11.1 2.8 %collective-permute-done.1 = bf16[7,144,128]{2,1,0:T(8,128)(2,1)S(1)} collective-permute-done((bf16[7,144,128]{2,1,0:T(8,128)(2,1)}, bf16[7,144,128]{2,1,0:T(8,128)(2,1)S(1)}, u32[]{:S(2)}, u32[]{:S(2)}) %collective-permute-start.1) | collective-permute-done | bytes 258080 | tf_op jit(solution)/shard_map/ppermute | solution.py:488
  13.9 4.2 %collective-permute-done = bf16[7,144,128]{2,1,0:T(8,128)(2,1)S(1)} collective-permute-done((bf16[7,144,128]{2,1,0:T(8,128)(2,1)}, bf16[7,144,128]{2,1,0:T(8,128)(2,1)S(1)}, u32[]{:S(2)}, u32[]{:S(2)}) %collective-permute-start) | collective-permute-done | bytes 258080 | tf_op jit(solution)/shard_map/ppermute | solution.py:488
  18.2 0.0 copy-done.6
  18.2 0.0 copy-start.7
  18.3 0.0 copy-start
  18.3 0.4 collective-permute-start.5
  18.7 3.6 %collective-permute-start.4 = (bf16[21,144,128]{2,1,0:T(8,128)(2,1)S(1)}, bf16[21,144,128]{2,1,0:T(8,128)(2,1)S(1)}, u32[]{:S(2)}, u32[]{:S(2)}) collective-permute-start(bf16[21,144,128]{2,1,0:T(8,128)(2,1)S(1)} %constant_dynamic-update-slice_fusion.refs_1_), channel_id=1, source_target_pairs={{0,8},{8,16},{16,24},{24,32},{32,40},{40,48},{48,56},{56,64},{64,7... | collective-permute-start | bytes 2322440 | tf_op jit(solution)/shard_map/ppermute | solution.py:488
  22.3 1.4 %collective-permute-start.7 = (bf16[9,144,128]{2,1,0:T(8,128)(2,1)S(1)}, bf16[9,144,128]{2,1,0:T(8,128)(2,1)S(1)}, u32[]{:S(2)}, u32[]{:S(2)}) collective-permute-start(bf16[9,144,128]{2,1,0:T(8,128)(2,1)S(1)} %select_select_fusion.refs_4_), channel_id=1, source_target_pairs={{0,7},{1,0},{2,1},{3,2},{4,3},{5,4},{6,5},{7,6},{8,15},{9,8},{10,9... | collective-permute-start | bytes 995336 | tf_op jit(solution)/shard_map/ppermute | solution.py:488
  23.7 3.0 %collective-permute-start.6 = (bf16[9,144,128]{2,1,0:T(8,128)(2,1)S(1)}, bf16[9,144,128]{2,1,0:T(8,128)(2,1)S(1)}, u32[]{:S(2)}, u32[]{:S(2)}) collective-permute-start(bf16[9,144,128]{2,1,0:T(8,128)(2,1)S(1)} %select_select_fusion.refs_4_), channel_id=1, source_target_pairs={{0,1},{1,2},{2,3},{3,4},{4,5},{5,6},{6,7},{7,0},{8,9},{9,10},{10,1... | collective-permute-start | bytes 995336 | tf_op jit(solution)/shard_map/ppermute | solution.py:488
  26.7 0.7 copy.12.lists_ref
  27.4 0.0 copy-done.8
  27.4 0.7 copy.11.head_ref
  28.1 2.0 %weights.1 = (bf16[128,256]{1,0:T(8,128)(2,1)}, bf16[512,128]{1,0:T(8,128)(2,1)}, f32[512,128]{1,0:T(8,128)}, bf16[64,512]{1,0:T(8,128)(2,1)}) custom-call(bf16[128,128]{1,0:T(8,128)(2,1)} %key_ref.1, bf16[128,128]{1,0:T(8,128)(2,1)} %value_ref.1, bf16[16,64]{1,0:T(8,128)(2,1)} %radial_ref.1, f32[1,64]{1,0:T(1,128)} %bitcast.14, bf16[64,8]{1,0:T(8,128)(2,1)} %copy.11.head_ref), custom_call_target="tpu_custom_call" | custom-call | tf_op jit(solution)/shard_map/weights/pallas_call | solution.py:105
  30.1 4.2 %collective-permute-done.7.refs_5_ = bf16[9,144,128]{2,1,0:T(8,128)(2,1)S(1)} collective-permute-done((bf16[9,144,128]{2,1,0:T(8,128)(2,1)S(1)}, bf16[9,144,128]{2,1,0:T(8,128)(2,1)S(1)}, u32[]{:S(2)}, u32[]{:S(2)}) %collective-permute-start.7) | collective-permute-done | bytes 331808 | tf_op jit(solution)/shard_map/ppermute | solution.py:488
  34.3 6.1 %collective-permute-done.6.refs_3_ = bf16[9,144,128]{2,1,0:T(8,128)(2,1)S(1)} collective-permute-done((bf16[9,144,128]{2,1,0:T(8,128)(2,1)S(1)}, bf16[9,144,128]{2,1,0:T(8,128)(2,1)S(1)}, u32[]{:S(2)}, u32[]{:S(2)}) %collective-permute-start.6) | collective-permute-done | bytes 331808 | tf_op jit(solution)/shard_map/ppermute | solution.py:488
  40.4 0.0 collective-permute-done.5.refs_2_
  40.4 0.0 collective-permute-done.4.refs_0_
  40.5 0.7 copy-done.5
  41.2 0.2 copy-done.2
  41.4 0.2 copy-done.3
  41.6 71.2 %attend.1 = bf16[2048,128]{1,0:T(8,128)(2,1)} custom-call(s32[1,16]{1,0:T(1,128)} %bitcast.13, s32[1]{0:T(128)} %bitcast.1.row_ref, s32[16,4]{1,0:T(8,128)} %copy.12.lists_ref, bf16[21,144,128]{2,1,0:T(8,128)(2,1)} %copy-done.3, bf16[21,144,128]{2,1,0:T(8,128)(2,1)} %copy-done, bf16[21,144,128]{2,1,0:T(8,128)(2,1)} %copy-done.2, ...), custom_call_target="tpu_custom_call" | custom-call | tf_op jit(solution)/shard_map/attend/pallas_call | solution.py:457
  (15 shorter events, 0.1 us)
Async XLA Ops:
  1.9 6.3 %collective-permute-start.3 = (bf16[9,144,128]{2,1,0:T(8,128)(2,1)}, bf16[9,144,128]{2,1,0:T(8,128)(2,1)S(1)}, u32[]{:S(2)}, u32[]{:S(2)}) collective-permute-start(bf16[9,144,128]{2,1,0:T(8,128)(2,1)} %get-tuple-element.14), channel_id=1, source_target_pairs={{0,120},{8,0},{16,8},{24,16},{32,24},{40,32},{48,40},{56,48},{64,5... | collective-permute-start | bytes 995336 | tf_op jit(solution)/shard_map/ppermute | solution.py:488
  1.9 6.8 %collective-permute-start.2 = (bf16[9,144,128]{2,1,0:T(8,128)(2,1)}, bf16[9,144,128]{2,1,0:T(8,128)(2,1)S(1)}, u32[]{:S(2)}, u32[]{:S(2)}) collective-permute-start(bf16[9,144,128]{2,1,0:T(8,128)(2,1)} %get-tuple-element.14), channel_id=1, source_target_pairs={{0,8},{8,16},{16,24},{24,32},{32,40},{40,48},{48,56},{56,64},{64,7... | collective-permute-start | bytes 995336 | tf_op jit(solution)/shard_map/ppermute | solution.py:488
  2.4 11.5 %collective-permute-start.1 = (bf16[7,144,128]{2,1,0:T(8,128)(2,1)}, bf16[7,144,128]{2,1,0:T(8,128)(2,1)S(1)}, u32[]{:S(2)}, u32[]{:S(2)}) collective-permute-start(bf16[7,144,128]{2,1,0:T(8,128)(2,1)} %get-tuple-element.13), channel_id=1, source_target_pairs={{0,7},{1,0},{2,1},{3,2},{4,3},{5,4},{6,5},{7,6},{8,15},{9,8},{10,9... | collective-permute-start | bytes 774152 | tf_op jit(solution)/shard_map/ppermute | solution.py:488
  3.8 14.3 %collective-permute-start = (bf16[7,144,128]{2,1,0:T(8,128)(2,1)}, bf16[7,144,128]{2,1,0:T(8,128)(2,1)S(1)}, u32[]{:S(2)}, u32[]{:S(2)}) collective-permute-start(bf16[7,144,128]{2,1,0:T(8,128)(2,1)} %get-tuple-element.13), channel_id=1, source_target_pairs={{0,1},{1,2},{2,3},{3,4},{4,5},{5,6},{6,7},{7,0},{8,9},{9,10},{10,1... | collective-permute-start | bytes 774152 | tf_op jit(solution)/shard_map/ppermute | solution.py:488
  6.8 0.7 copy-start.9
  11.1 12.6 %copy-start.1 = (bf16[9,144,128]{2,1,0:T(8,128)(2,1)}, bf16[9,144,128]{2,1,0:T(8,128)(2,1)S(1)}, u32[]{:S(2)}) copy-start(bf16[9,144,128]{2,1,0:T(8,128)(2,1)S(1)} %select_select_fusion.refs_4_) | copy-start | bytes 995332
  11.1 7.1 %copy-start.6 = (bf16[7,144,128]{2,1,0:T(8,128)(2,1)S(1)}, bf16[7,144,128]{2,1,0:T(8,128)(2,1)}, u32[]{:S(2)}) copy-start(bf16[7,144,128]{2,1,0:T(8,128)(2,1)} %get-tuple-element.13) | copy-start | bytes 774148
  18.2 8.5 %copy-start.7 = (s32[1,1,16,4]{2,3,1,0:T(4,128)S(1)}, s32[1,1,16,4]{2,3,1,0:T(4,128)}, u32[]{:S(2)}) copy-start(s32[1,1,16,4]{2,3,1,0:T(4,128)} %param.13) | copy-start | bytes 772
  18.3 22.1 %copy-start = (bf16[21,144,128]{2,1,0:T(8,128)(2,1)}, bf16[21,144,128]{2,1,0:T(8,128)(2,1)S(1)}, u32[]{:S(2)}) copy-start(bf16[21,144,128]{2,1,0:T(8,128)(2,1)S(1)} %constant_dynamic-update-slice_fusion.refs_1_) | copy-start | bytes 2322436
  18.3 22.1 %collective-permute-start.5 = (bf16[21,144,128]{2,1,0:T(8,128)(2,1)S(1)}, bf16[21,144,128]{2,1,0:T(8,128)(2,1)S(1)}, u32[]{:S(2)}, u32[]{:S(2)}) collective-permute-start(bf16[21,144,128]{2,1,0:T(8,128)(2,1)S(1)} %constant_dynamic-update-slice_fusion.refs_1_), channel_id=1, source_target_pairs={{0,120},{8,0},{16,8},{24,16},{32,24},{40,32},{48,40},{56,48},{64,5... | collective-permute-start | bytes 2322440 | tf_op jit(solution)/shard_map/ppermute | solution.py:488
  18.7 21.7 %collective-permute-start.4 = (bf16[21,144,128]{2,1,0:T(8,128)(2,1)S(1)}, bf16[21,144,128]{2,1,0:T(8,128)(2,1)S(1)}, u32[]{:S(2)}, u32[]{:S(2)}) collective-permute-start(bf16[21,144,128]{2,1,0:T(8,128)(2,1)S(1)} %constant_dynamic-update-slice_fusion.refs_1_), channel_id=1, source_target_pairs={{0,8},{8,16},{16,24},{24,32},{32,40},{40,48},{48,56},{56,64},{64,7... | collective-permute-start | bytes 2322440 | tf_op jit(solution)/shard_map/ppermute | solution.py:488
  22.3 12.0 %collective-permute-start.7 = (bf16[9,144,128]{2,1,0:T(8,128)(2,1)S(1)}, bf16[9,144,128]{2,1,0:T(8,128)(2,1)S(1)}, u32[]{:S(2)}, u32[]{:S(2)}) collective-permute-start(bf16[9,144,128]{2,1,0:T(8,128)(2,1)S(1)} %select_select_fusion.refs_4_), channel_id=1, source_target_pairs={{0,7},{1,0},{2,1},{3,2},{4,3},{5,4},{6,5},{7,6},{8,15},{9,8},{10,9... | collective-permute-start | bytes 995336 | tf_op jit(solution)/shard_map/ppermute | solution.py:488
  23.7 16.7 %collective-permute-start.6 = (bf16[9,144,128]{2,1,0:T(8,128)(2,1)S(1)}, bf16[9,144,128]{2,1,0:T(8,128)(2,1)S(1)}, u32[]{:S(2)}, u32[]{:S(2)}) collective-permute-start(bf16[9,144,128]{2,1,0:T(8,128)(2,1)S(1)} %select_select_fusion.refs_4_), channel_id=1, source_target_pairs={{0,1},{1,2},{2,3},{3,4},{4,5},{5,6},{6,7},{7,0},{8,9},{9,10},{10,1... | collective-permute-start | bytes 995336 | tf_op jit(solution)/shard_map/ppermute | solution.py:488
  26.7 0.7 copy-start.8
  34.3 6.1 %copy-start.4 = (bf16[9,144,128]{2,1,0:T(8,128)(2,1)}, bf16[9,144,128]{2,1,0:T(8,128)(2,1)S(1)}, u32[]{:S(2)}) copy-start(bf16[9,144,128]{2,1,0:T(8,128)(2,1)S(1)} %collective-permute-done.7.refs_5_) | copy-start | bytes 995332
  40.4 0.7 copy-start.5
  40.4 1.0 copy-start.2
  40.4 1.2 %copy-start.3 = (bf16[21,144,128]{2,1,0:T(8,128)(2,1)}, bf16[21,144,128]{2,1,0:T(8,128)(2,1)S(1)}, u32[]{:S(2)}) copy-start(bf16[21,144,128]{2,1,0:T(8,128)(2,1)S(1)} %collective-permute-done.4.refs_0_) | copy-start | bytes 2322436

commit v2 on v1

--- a/solution.py
+++ b/solution.py
@@ -497,14 +497,12 @@
     place = (counts.T, row[None])
     light, extra = make_payload(*place, features[0, 0], positions.transpose(0, 2, 1, 3)[0])
     dense = line > LIGHT_BLOCKS * ATOM_BLOCK
+    before, after = shift(extra, "gx", 1), shift(extra, "gx", -1)
     extra = jnp.where(
-        dense[(row - 1) % rows],
-        shift(extra, "gx", 1),
-        jnp.where(dense[(row + 1) % rows], shift(extra, "gx", -1), extra),
+        dense[(row - 1) % rows], before, jnp.where(dense[(row + 1) % rows], after, extra)
     )
     low, high = shift(light, "gy", 1), shift(light, "gy", -1)
     further = [shift(extra, "gy", 1), extra, shift(extra, "gy", -1)]
-    low, high, _ = lax.optimization_barrier((low, high, extra))
     column = jnp.concatenate([low, light, high], 0)
     srcs = [shift(column, "gx", 1), column, shift(column, "gx", -1)] + further
     wkv, w1, b1, w2 = make_weights(w_key, w_value, w_radial, b_radial, w_head)

time: 113 us -> 114 us (level)
  waiting for transfers between devices: 17.9 us -> 24.6 us
  starting transfers between devices: 13.4 us -> 9.11 us
    ppermute x8, waiting for transfers between devices: 17.9 us -> 24.6 us  [shift(): return lax.ppermute(x, axis, [(i, (i + by) % size) for i in range(size)])]
    ppermute x8, starting transfers between devices: 13.4 us -> 9.11 us  [shift(): return lax.ppermute(x, axis, [(i, (i + by) % size) for i in range(size)])]
    unnamed x23 -> x25, local copies, waits for them, and re-layouts: 2.63 us -> 2.04 us
  transfers between devices with their start and end apart: 8 -> 8, of which waited for: 5 -> 4; matrix products, arithmetic and copies ran while one was open for 4% -> 3% of each run, Pallas kernels for 2% -> 2%
where the time goes in v2:
time: 114 us
  Pallas kernels  75.1 us (66%)
  waiting for transfers between devices  24.6 us (22%)
  starting transfers between devices  9.11 us (8%)
  local copies, waits for them, and re-layouts  3.4 us (3%)
  other arithmetic  1.35 us (1%)
    pallas_call x1, Pallas kernels, attend(): pl.pallas_call(attend_kernel, out_shape=jax.ShapeDtypeStruct((slots, chan...  71.2 us
    ppermute x8, waiting for transfers between devices, shift(): return lax.ppermute(x, axis, [(i, (i + by) % size) for i in range(size)])  24.6 us
    ppermute x8, starting transfers between devices, shift(): return lax.ppermute(x, axis, [(i, (i + by) % size) for i in range(size)])  9.11 us
  transfers between devices with their start and end apart: 8, of which 4 were waited for; matrix products, arithmetic and copies ran while one was open for 3% of the time, Pallas kernels for 2%

profile of v2, /device:TPU:118, one launch (start us, length us, event | category | flops | bytes accessed | tf_op | source)
XLA Modules:
  0.0 113.7 jit_solution(4764586276656529725)
XLA Ops:
  0.0 1.9 %payload.1 = (bf16[7,144,128]{2,1,0:T(8,128)(2,1)}, bf16[9,144,128]{2,1,0:T(8,128)(2,1)}) custom-call(s32[1,16]{1,0:T(1,128)} %bitcast.12, s32[1]{0:T(128)} %bitcast.1.row_ref, bf16[2048,128]{1,0:T(8,128)(2,1)} %bitcast.9, f32[3,1,2048]{2,1,0:T(1,128)} %bitcast.10), custom_call_target="tpu_custom_call" | custom-call | tf_op jit(solution)/shard_map/payload/pallas_call | solution.py:52
  1.9 2.1 %collective-permute-start = (bf16[7,144,128]{2,1,0:T(8,128)(2,1)}, bf16[7,144,128]{2,1,0:T(8,128)(2,1)S(1)}, u32[]{:S(2)}, u32[]{:S(2)}) collective-permute-start(bf16[7,144,128]{2,1,0:T(8,128)(2,1)} %get-tuple-element.11), channel_id=1, source_target_pairs={{0,1},{1,2},{2,3},{3,4},{4,5},{5,6},{6,7},{7,0},{8,9},{9,10},{10,1... | collective-permute-start | bytes 774152 | tf_op jit(solution)/shard_map/ppermute | solution.py:488
  4.0 1.4 %collective-permute-start.1 = (bf16[7,144,128]{2,1,0:T(8,128)(2,1)}, bf16[7,144,128]{2,1,0:T(8,128)(2,1)S(1)}, u32[]{:S(2)}, u32[]{:S(2)}) collective-permute-start(bf16[7,144,128]{2,1,0:T(8,128)(2,1)} %get-tuple-element.11), channel_id=1, source_target_pairs={{0,7},{1,0},{2,1},{3,2},{4,3},{5,4},{6,5},{7,6},{8,15},{9,8},{10,9... | collective-permute-start | bytes 774152 | tf_op jit(solution)/shard_map/ppermute | solution.py:488
  5.4 0.0 collective-permute-start.5
  5.4 0.5 collective-permute-start.4
  5.9 6.8 %collective-permute-done = bf16[7,144,128]{2,1,0:T(8,128)(2,1)S(1)} collective-permute-done((bf16[7,144,128]{2,1,0:T(8,128)(2,1)}, bf16[7,144,128]{2,1,0:T(8,128)(2,1)S(1)}, u32[]{:S(2)}, u32[]{:S(2)}) %collective-permute-start) | collective-permute-done | bytes 258080 | tf_op jit(solution)/shard_map/ppermute | solution.py:488
  12.7 0.0 copy-done.7
  12.8 0.0 copy-start.10
  12.8 0.0 copy-start.6
  12.8 6.1 %collective-permute-done.1 = bf16[7,144,128]{2,1,0:T(8,128)(2,1)S(1)} collective-permute-done((bf16[7,144,128]{2,1,0:T(8,128)(2,1)}, bf16[7,144,128]{2,1,0:T(8,128)(2,1)S(1)}, u32[]{:S(2)}, u32[]{:S(2)}) %collective-permute-start.1) | collective-permute-done | bytes 258080 | tf_op jit(solution)/shard_map/ppermute | solution.py:488
  19.0 0.1 collective-permute-start.3
  19.1 0.5 collective-permute-start.2
  19.6 0.0 copy-done.10
  19.6 0.6 constant_dynamic-slice_fusion.1
  20.2 0.0 collective-permute-done.5
  20.2 0.0 collective-permute-done.4
  20.3 0.0 copy-start.8
  20.3 1.3 %select_select_fusion.refs_4_ = bf16[9,144,128]{2,1,0:T(8,128)(2,1)S(1)} fusion(bf16[9,144,128]{2,1,0:T(8,128)(2,1)S(1)} %collective-permute-done.4, bf16[9,144,128]{2,1,0:T(8,128)(2,1)S(1)} %collective-permute-done.5, bf16[9,144,128]{2,1,0:T(8,128)(2,1)S(1)} %copy-done.6, pred[]{:T(512)} %bitcast.6, pred[]{:T(512)} %bitcast.5), kind=kLoop, calls=%fused_computation | loop fusion | flops 331776 | bytes 1327106 | tf_op jit(solution)/shard_map/jit(_where)/select_n | solution.py:501
  21.6 1.5 %collective-permute-start.7 = (bf16[9,144,128]{2,1,0:T(8,128)(2,1)S(1)}, bf16[9,144,128]{2,1,0:T(8,128)(2,1)S(1)}, u32[]{:S(2)}, u32[]{:S(2)}) collective-permute-start(bf16[9,144,128]{2,1,0:T(8,128)(2,1)S(1)} %select_select_fusion.refs_4_), channel_id=1, source_target_pairs={{0,7},{1,0},{2,1},{3,2},{4,3},{5,4},{6,5},{7,6},{8,15},{9,8},{10,9... | collective-permute-start | bytes 995336 | tf_op jit(solution)/shard_map/ppermute | solution.py:488
  23.1 3.0 %collective-permute-start.6 = (bf16[9,144,128]{2,1,0:T(8,128)(2,1)S(1)}, bf16[9,144,128]{2,1,0:T(8,128)(2,1)S(1)}, u32[]{:S(2)}, u32[]{:S(2)}) collective-permute-start(bf16[9,144,128]{2,1,0:T(8,128)(2,1)S(1)} %select_select_fusion.refs_4_), channel_id=1, source_target_pairs={{0,1},{1,2},{2,3},{3,4},{4,5},{5,6},{6,7},{7,0},{8,9},{9,10},{10,1... | collective-permute-start | bytes 995336 | tf_op jit(solution)/shard_map/ppermute | solution.py:488
  26.1 0.7 copy.12.lists_ref
  26.8 0.0 copy-done.9
  26.8 0.7 copy.11.head_ref
  27.5 2.0 %weights.1 = (bf16[128,256]{1,0:T(8,128)(2,1)}, bf16[512,128]{1,0:T(8,128)(2,1)}, f32[512,128]{1,0:T(8,128)}, bf16[64,512]{1,0:T(8,128)(2,1)}) custom-call(bf16[128,128]{1,0:T(8,128)(2,1)} %key_ref.1, bf16[128,128]{1,0:T(8,128)(2,1)} %value_ref.1, bf16[16,64]{1,0:T(8,128)(2,1)} %radial_ref.1, f32[1,64]{1,0:T(1,128)} %bitcast.14, bf16[64,8]{1,0:T(8,128)(2,1)} %copy.11.head_ref), custom_call_target="tpu_custom_call" | custom-call | tf_op jit(solution)/shard_map/weights/pallas_call | solution.py:105
  29.5 5.3 %collective-permute-done.7.refs_5_ = bf16[9,144,128]{2,1,0:T(8,128)(2,1)S(1)} collective-permute-done((bf16[9,144,128]{2,1,0:T(8,128)(2,1)S(1)}, bf16[9,144,128]{2,1,0:T(8,128)(2,1)S(1)}, u32[]{:S(2)}, u32[]{:S(2)}) %collective-permute-start.7) | collective-permute-done | bytes 331808 | tf_op jit(solution)/shard_map/ppermute | solution.py:488
  34.8 6.4 %collective-permute-done.6.refs_3_ = bf16[9,144,128]{2,1,0:T(8,128)(2,1)S(1)} collective-permute-done((bf16[9,144,128]{2,1,0:T(8,128)(2,1)S(1)}, bf16[9,144,128]{2,1,0:T(8,128)(2,1)S(1)}, u32[]{:S(2)}, u32[]{:S(2)}) %collective-permute-start.6) | collective-permute-done | bytes 331808 | tf_op jit(solution)/shard_map/ppermute | solution.py:488
  41.1 0.0 collective-permute-done.3.refs_2_
  41.2 0.0 collective-permute-done.2.refs_0_
  41.2 0.7 copy-done.5
  41.9 0.3 copy-done.2
  42.1 0.3 copy-done.3
  42.4 71.2 %attend.1 = bf16[2048,128]{1,0:T(8,128)(2,1)} custom-call(s32[1,16]{1,0:T(1,128)} %bitcast.13, s32[1]{0:T(128)} %bitcast.1.row_ref, s32[16,4]{1,0:T(8,128)} %copy.12.lists_ref, bf16[21,144,128]{2,1,0:T(8,128)(2,1)} %copy-done.3, bf16[21,144,128]{2,1,0:T(8,128)(2,1)} %copy-done, bf16[21,144,128]{2,1,0:T(8,128)(2,1)} %copy-done.2, ...), custom_call_target="tpu_custom_call" | custom-call | tf_op jit(solution)/shard_map/attend/pallas_call | solution.py:457
  (17 shorter events, 0.1 us)
Async XLA Ops:
  1.9 10.8 %collective-permute-start = (bf16[7,144,128]{2,1,0:T(8,128)(2,1)}, bf16[7,144,128]{2,1,0:T(8,128)(2,1)S(1)}, u32[]{:S(2)}, u32[]{:S(2)}) collective-permute-start(bf16[7,144,128]{2,1,0:T(8,128)(2,1)} %get-tuple-element.11), channel_id=1, source_target_pairs={{0,1},{1,2},{2,3},{3,4},{4,5},{5,6},{6,7},{7,0},{8,9},{9,10},{10,1... | collective-permute-start | bytes 774152 | tf_op jit(solution)/shard_map/ppermute | solution.py:488
  4.0 14.9 %collective-permute-start.1 = (bf16[7,144,128]{2,1,0:T(8,128)(2,1)}, bf16[7,144,128]{2,1,0:T(8,128)(2,1)S(1)}, u32[]{:S(2)}, u32[]{:S(2)}) collective-permute-start(bf16[7,144,128]{2,1,0:T(8,128)(2,1)} %get-tuple-element.11), channel_id=1, source_target_pairs={{0,7},{1,0},{2,1},{3,2},{4,3},{5,4},{6,5},{7,6},{8,15},{9,8},{10,9... | collective-permute-start | bytes 774152 | tf_op jit(solution)/shard_map/ppermute | solution.py:488
  5.4 14.8 %collective-permute-start.5 = (bf16[9,144,128]{2,1,0:T(8,128)(2,1)}, bf16[9,144,128]{2,1,0:T(8,128)(2,1)S(1)}, u32[]{:S(2)}, u32[]{:S(2)}) collective-permute-start(bf16[9,144,128]{2,1,0:T(8,128)(2,1)} %get-tuple-element.12), channel_id=1, source_target_pairs={{0,120},{8,0},{16,8},{24,16},{32,24},{40,32},{48,40},{56,48},{64,5... | collective-permute-start | bytes 995336 | tf_op jit(solution)/shard_map/ppermute | solution.py:488
  5.4 14.8 %collective-permute-start.4 = (bf16[9,144,128]{2,1,0:T(8,128)(2,1)}, bf16[9,144,128]{2,1,0:T(8,128)(2,1)S(1)}, u32[]{:S(2)}, u32[]{:S(2)}) collective-permute-start(bf16[9,144,128]{2,1,0:T(8,128)(2,1)} %get-tuple-element.12), channel_id=1, source_target_pairs={{0,8},{8,16},{16,24},{24,32},{32,40},{40,48},{48,56},{56,64},{64,7... | collective-permute-start | bytes 995336 | tf_op jit(solution)/shard_map/ppermute | solution.py:488
  5.9 6.8 %copy-start.7 = (bf16[7,144,128]{2,1,0:T(8,128)(2,1)S(1)}, bf16[7,144,128]{2,1,0:T(8,128)(2,1)}, u32[]{:S(2)}) copy-start(bf16[7,144,128]{2,1,0:T(8,128)(2,1)} %get-tuple-element.11) | copy-start | bytes 774148
  12.8 6.8 %copy-start.10 = (s32[16,1]{0,1:T(1,128)S(1)}, s32[16,1]{0,1:T(1,128)}, u32[]{:S(2)}) copy-start(s32[16,1]{0,1:T(1,128)} %param.12) | copy-start | bytes 196
  12.8 7.5 %copy-start.6 = (bf16[9,144,128]{2,1,0:T(8,128)(2,1)S(1)}, bf16[9,144,128]{2,1,0:T(8,128)(2,1)}, u32[]{:S(2)}) copy-start(bf16[9,144,128]{2,1,0:T(8,128)(2,1)} %get-tuple-element.12) | copy-start | bytes 995332
  19.0 22.2 %copy-start = (bf16[21,144,128]{2,1,0:T(8,128)(2,1)}, bf16[21,144,128]{2,1,0:T(8,128)(2,1)S(1)}, u32[]{:S(2)}) copy-start(bf16[21,144,128]{2,1,0:T(8,128)(2,1)S(1)} %constant_dynamic-update-slice_fusion.refs_1_) | copy-start | bytes 2322436
  19.0 22.1 %collective-permute-start.3 = (bf16[21,144,128]{2,1,0:T(8,128)(2,1)S(1)}, bf16[21,144,128]{2,1,0:T(8,128)(2,1)S(1)}, u32[]{:S(2)}, u32[]{:S(2)}) collective-permute-start(bf16[21,144,128]{2,1,0:T(8,128)(2,1)S(1)} %constant_dynamic-update-slice_fusion.refs_1_), channel_id=1, source_target_pairs={{0,120},{8,0},{16,8},{24,16},{32,24},{40,32},{48,40},{56,48},{64,5... | collective-permute-start | bytes 2322440 | tf_op jit(solution)/shard_map/ppermute | solution.py:488
  19.1 22.1 %collective-permute-start.2 = (bf16[21,144,128]{2,1,0:T(8,128)(2,1)S(1)}, bf16[21,144,128]{2,1,0:T(8,128)(2,1)S(1)}, u32[]{:S(2)}, u32[]{:S(2)}) collective-permute-start(bf16[21,144,128]{2,1,0:T(8,128)(2,1)S(1)} %constant_dynamic-update-slice_fusion.refs_1_), channel_id=1, source_target_pairs={{0,8},{8,16},{16,24},{24,32},{32,40},{40,48},{48,56},{56,64},{64,7... | collective-permute-start | bytes 2322440 | tf_op jit(solution)/shard_map/ppermute | solution.py:488
  20.3 5.9 %copy-start.8 = (s32[1,1,16,4]{2,3,1,0:T(4,128)S(1)}, s32[1,1,16,4]{2,3,1,0:T(4,128)}, u32[]{:S(2)}) copy-start(s32[1,1,16,4]{2,3,1,0:T(4,128)} %param.13) | copy-start | bytes 772
  21.6 19.6 %copy-start.1 = (bf16[9,144,128]{2,1,0:T(8,128)(2,1)}, bf16[9,144,128]{2,1,0:T(8,128)(2,1)S(1)}, u32[]{:S(2)}) copy-start(bf16[9,144,128]{2,1,0:T(8,128)(2,1)S(1)} %select_select_fusion.refs_4_) | copy-start | bytes 995332
  21.6 13.1 %collective-permute-start.7 = (bf16[9,144,128]{2,1,0:T(8,128)(2,1)S(1)}, bf16[9,144,128]{2,1,0:T(8,128)(2,1)S(1)}, u32[]{:S(2)}, u32[]{:S(2)}) collective-permute-start(bf16[9,144,128]{2,1,0:T(8,128)(2,1)S(1)} %select_select_fusion.refs_4_), channel_id=1, source_target_pairs={{0,7},{1,0},{2,1},{3,2},{4,3},{5,4},{6,5},{7,6},{8,15},{9,8},{10,9... | collective-permute-start | bytes 995336 | tf_op jit(solution)/shard_map/ppermute | solution.py:488
  23.1 18.1 %collective-permute-start.6 = (bf16[9,144,128]{2,1,0:T(8,128)(2,1)S(1)}, bf16[9,144,128]{2,1,0:T(8,128)(2,1)S(1)}, u32[]{:S(2)}, u32[]{:S(2)}) collective-permute-start(bf16[9,144,128]{2,1,0:T(8,128)(2,1)S(1)} %select_select_fusion.refs_4_), channel_id=1, source_target_pairs={{0,1},{1,2},{2,3},{3,4},{4,5},{5,6},{6,7},{7,0},{8,9},{9,10},{10,1... | collective-permute-start | bytes 995336 | tf_op jit(solution)/shard_map/ppermute | solution.py:488
  26.1 0.7 copy-start.9
  34.8 6.4 %copy-start.4 = (bf16[9,144,128]{2,1,0:T(8,128)(2,1)}, bf16[9,144,128]{2,1,0:T(8,128)(2,1)S(1)}, u32[]{:S(2)}) copy-start(bf16[9,144,128]{2,1,0:T(8,128)(2,1)S(1)} %collective-permute-done.7.refs_5_) | copy-start | bytes 995332
  41.1 0.7 copy-start.5
  41.2 1.0 copy-start.2
  41.2 1.3 %copy-start.3 = (bf16[21,144,128]{2,1,0:T(8,128)(2,1)}, bf16[21,144,128]{2,1,0:T(8,128)(2,1)S(1)}, u32[]{:S(2)}) copy-start(bf16[21,144,128]{2,1,0:T(8,128)(2,1)S(1)} %collective-permute-done.2.refs_0_) | copy-start | bytes 2322436
